TPU v7x, 256 devices: a whole 4x4x8 slice. The times are simulated.
256 devices in a mesh: prefix: 8 (over z), feat: 32 (over y, x, core).
Axes of the slice: x: 4, y: 4, z: 8, core: 2. Of those that a mesh axis runs over, the one named last changes fastest.
Arguments:
- activations: float32 [1024, 1152], P('feat'), may hold values from -6 to 6
- enc_weight: float32 [16, 9216, 1152], P('prefix', 'feat'), may hold values from -0.1875 to 0.1875
- dec_weight: float32 [16, 9216, 1152], P('prefix', 'feat'), may hold values from -0.0625 to 0.0625
Outputs:
- enc_grad: float32 [16, 9216, 1152], P('prefix', 'feat')
- dec_grad: float32 [16, 9216, 1152], P('prefix', 'feat')
All inputs are finite; a program needn't handle non-finite values.
Results may differ from a plain program's by a relative error of at most 0.000094.
Values sent between devices are 32-bit elements; how exact they have to be, the bound alone decides.
No kernel may reach another device: no remote copies, remote signals or barrier semaphores. Data moves between devices by JAX's collectives and lax.ppermute only.
A program may use at most 128 MiB of HBM per device.

v0:
```python
import jax
import jax.numpy as jnp
from jax import lax
from jax.sharding import PartitionSpec as P

HIGHEST = lax.Precision.HIGHEST


def entering(shard, axis, combine, identity, reverse):
    count, here = (lax.axis_size(axis), lax.axis_index(axis))
    everything = lax.all_gather(shard, axis)
    start = jnp.broadcast_to(jnp.asarray(identity, shard.dtype), shard.shape)

    def step(k, before):
        at = count - 1 - k if reverse else k
        reached = at > here if reverse else at < here
        new = combine(before, everything[at])
        return jnp.where(reached, new, before)

    return lax.fori_loop(0, count, step, start)


def add_terms(earlier, later):
    return earlier + later


def chain_scan(decoded, act_rows):
    group_total = jnp.sum(decoded, axis=1)
    nothing = jnp.zeros_like(group_total)
    before = entering(group_total, "prefix", add_terms, nothing, False)
    rebuilt = before[:, None, :] + jnp.cumsum(decoded, axis=1)
    errors = rebuilt - act_rows[:, None, :]
    error_total = jnp.sum(errors, axis=1)
    beyond = entering(error_total, "prefix", add_terms, nothing, True)
    return beyond[:, None, :] + jnp.flip(jnp.cumsum(jnp.flip(errors, 1), axis=1), 1)


def per_device(activations, enc_weight, dec_weight):
    local_groups, local_feats, model_width = enc_weight.shape
    gathered = lax.all_gather(activations, "feat", axis=0, tiled=True)
    tokens = gathered.shape[0]
    pre_act = jnp.einsum("nd,gkd->gnk", gathered, enc_weight, precision=HIGHEST)
    features = jax.nn.softplus(4.0 * pre_act) / 4.0
    slopes = jax.nn.sigmoid(4.0 * pre_act)
    factor = 2.0 / tokens
    empty = jnp.zeros(enc_weight.shape, jnp.float32)
    own_rows = tokens // lax.axis_size("feat")
    feat_rows = features
    product = jnp.einsum("gnk,gkd->ngd", feat_rows, dec_weight, precision=HIGHEST)
    summed = lax.psum_scatter(
        product.reshape(lax.axis_size("feat") * own_rows, local_groups * model_width),
        "feat",
        scatter_dimension=0,
        tiled=True,
    )
    decoded = summed.reshape(summed.shape[0], local_groups, model_width)
    suffix = factor * chain_scan(decoded, activations)
    suffix_piece = lax.all_gather(suffix, "feat", axis=0, tiled=True)
    feat_rows = features
    dec_new = empty + jnp.einsum("gnk,ngd->gkd", feat_rows, suffix_piece, precision=HIGHEST)
    gate = jnp.einsum("ngd,gkd->gnk", suffix_piece, dec_weight, precision=HIGHEST) * slopes
    enc_new = empty + jnp.einsum("gnk,nd->gkd", gate, gathered, precision=HIGHEST)
    return (enc_new, dec_new)


def solution(mesh):
    in_specs = (P("feat", None), P("prefix", "feat", None), P("prefix", "feat", None))
    out_specs = (P("prefix", "feat", None), P("prefix", "feat", None))
    return jax.shard_map(
        per_device, mesh=mesh, in_specs=in_specs, out_specs=out_specs, check_vma=False
    )
```

profile of v0, /device:TPU:1, one launch (start us, length us, event | category | flops | bytes accessed | tf_op | source)
XLA Modules:
  0.0 425.4 jit_solution(15453496965193077454)
XLA Ops:
  7.2 0.0 copy-start
  7.2 0.0 all-gather.7.cloned.1.call-start
  7.2 0.7 all-gather.7.cloned.1.call-update
  7.9 0.0 reduce-scatter.4.cloned.1.call-start
  8.0 58.4 %all-gather.7.cloned.1.call-done = f32[1024,1152]{1,0:T(8,128)} async-done(((f32[32,1152]{1,0:T(8,128)}), f32[1024,1152]{1,0:T(8,128)}) %all-gather.7.cloned.1.call-update) | async-done | bytes 4718608 | tf_op jit(solution)/shard_map/all_gather | solution.py:40
  66.4 12.5 %fusion.2 = f32[2,288,1024]{2,1,0:T(8,128)S(1)} fusion(f32[2,288,1152]{2,1,0:T(8,128)} %param.8, f32[1024,1152]{1,0:T(8,128)} %all-gather.7.cloned.1.call-done), kind=kOutput, calls=%fused_computation.6 | convolution fusion | flops 8153726976 | bytes 9732096 | tf_op jit(solution)/shard_map/nd,gkd->gnk/dot_general | solution.py:42
  78.9 0.0 copy-start.2
  78.9 1.4 copy-done.2
  80.3 0.0 copy-done
  80.3 19.8 %convolution_bitcast_fusion = f32[1024,2,1152]{2,0,1:T(8,128)} fusion(f32[2,288,1152]{2,1,0:T(8,128)S(1)} %copy-done, f32[2,288,1024]{2,1,0:T(8,128)S(1)} %fusion.2), kind=kOutput, calls=%fused_computation.3 | convolution fusion | flops 8158445568 | bytes 14450688 | tf_op jit(solution)/shard_map/gnk,gkd->ngd/dot_general | solution.py:49
  100.1 9.6 %copy.8 = f32[1024,2,1152]{0,2,1:T(8,128)} copy(f32[1024,2,1152]{2,0,1:T(8,128)} %convolution_bitcast_fusion) | data formatting | bytes 18874368 | tf_op jit(solution)/shard_map/gnk,gkd->ngd/transpose | solution.py:49
  109.8 9.6 %copy.13 = f32[1024,2304]{1,0:T(8,128)} copy(f32[1024,2304]{0,1:T(8,128)} %bitcast.55) | data formatting | bytes 18874368
  119.4 0.0 reduce-scatter.4.cloned.1.call-update
  119.4 0.0 all-gather.11.cloned.1.call-start
  119.5 100.5 %reduce-scatter.4.cloned.1.call-done = f32[32,2304]{1,0:T(8,128)} async-done(((f32[1024,2304]{1,0:T(8,128)}), f32[32,2304]{1,0:T(8,128)}) %reduce-scatter.4.cloned.1.call-update) | async-done | bytes 294928
  219.9 2.3 copy.14
  222.3 1.4 reduce_sum.18
  223.7 0.0 copy-start.4
  223.7 0.9 copy.15
  224.6 0.0 all-gather.11.cloned.1.call-update
  224.6 0.0 all-gather.13.cloned.1.call-start
  224.7 1.6 copy.10
  226.3 33.4 %all-gather.11.cloned.1.call-done = f32[256,1152]{1,0:T(8,128)} async-done(((f32[32,1152]{1,0:T(8,128)}), f32[256,1152]{1,0:T(8,128)}) %all-gather.11.cloned.1.call-update) | async-done | bytes 1179664 | tf_op jit(solution)/shard_map/all_gather | solution.py:11
  259.7 7.8 %while.30 = (s32[]{:T(128)}, f32[32,1152]{1,0:T(8,128)S(1)}, s32[]{:T(128)}, f32[8,32,1152]{2,1,0:T(8,128)}, s32[]{:T(128)}, /*index=5*/s32[]{:T(128)}) while((s32[]{:T(128)}, f32[32,1152]{1,0:T(8,128)S(1)}, s32[]{:T(128)}, f32[8,32,1152]{2,1,0:T(8,128)}, s32[]{:T(128)}, /*index=5*/s32[]{:T(128)}) %tuple.89), condition=%wide.region_3.4_spmd.clone, body=%wide.region_2.3_spmd.clone.sunk | while | flops 110596 | bytes 442461 | solution.py:20
  259.7 1.0 add_select_fusion.4
  260.7 1.0 add_select_fusion.4
  261.7 1.0 add_select_fusion.4
  262.6 1.0 add_select_fusion.4
  263.6 1.0 add_select_fusion.4
  264.6 1.0 add_select_fusion.4
  265.6 1.0 add_select_fusion.4
  266.6 1.0 add_select_fusion.4
  267.5 0.0 copy-done.4
  267.5 0.9 fusion.29
  268.4 0.0 all-gather.13.cloned.1.call-update
  268.5 0.0 all-gather.9.cloned.1.call-start
  268.6 12.6 %fusion.30 = f32[32,2,1152]{2,0,1:T(8,128)S(1)} fusion(f32[32,2,1152]{2,0,1:T(8,128)S(1)} %rev.7), kind=kOutput, calls=%fused_computation.36 | output fusion | flops 73728 | bytes 589824 | tf_op jit(solution)/shard_map/jit(cumsum)/reduce_window_sum | solution.py:35
  281.1 24.7 %all-gather.13.cloned.1.call-done = f32[256,1152]{1,0:T(8,128)} async-done(((f32[32,1152]{1,0:T(8,128)}), f32[256,1152]{1,0:T(8,128)}) %all-gather.13.cloned.1.call-update) | async-done | bytes 1179664 | tf_op jit(solution)/shard_map/all_gather | solution.py:11
  305.9 7.9 %while.31 = (s32[]{:T(128)}, f32[32,1152]{1,0:T(8,128)S(1)}, s32[]{:T(128)}, f32[8,32,1152]{2,1,0:T(8,128)}, s32[]{:T(128)}, /*index=5*/s32[]{:T(128)}, s32[]{:T(128)}, s32[]{:T(128)}) while((s32[]{:T(128)}, f32[32,1152]{1,0:T(8,128)S(1)}, s32[]{:T(128)}, f32[8,32,1152]{2,1,0:T(8,128)}, s32[]{:T(128)}, /*index=5*/s32[]{:T(128)}, ...), condition=%wide.region_7.8_spmd.clone, body=%wide.region_6.7_spmd.clone.sunk | while | flops 110600 | bytes 442523 | solution.py:20
  305.9 1.0 add_select_fusion.5
  306.8 1.0 add_select_fusion.5
  307.8 1.0 add_select_fusion.5
  308.8 1.0 add_select_fusion.5
  309.8 1.0 add_select_fusion.5
  310.8 1.0 add_select_fusion.5
  311.8 1.0 add_select_fusion.5
  312.8 1.0 add_select_fusion.5
  313.7 0.7 add_multiply_fusion
  314.5 0.0 all-gather.9.cloned.1.call-update
  314.5 64.2 %all-gather.9.cloned.1.call-done = f32[1024,2,1152]{2,0,1:T(8,128)} async-done(((f32[32,2,1152]{2,0,1:T(8,128)}), f32[1024,2,1152]{2,0,1:T(8,128)}) %all-gather.9.cloned.1.call-update) | async-done | bytes 9437200 | tf_op jit(solution)/shard_map/all_gather | solution.py:58
  378.7 0.0 copy-start.1
  378.7 0.0 copy-start.3
  378.7 13.4 %fusion.31 = f32[2,1024,288]{1,2,0:T(8,128)S(1)} fusion(f32[1024,2,1152]{2,0,1:T(8,128)} %all-gather.9.cloned.1.call-done, f32[2,288,1152]{2,1,0:T(8,128)S(1)} %copy-done), kind=kOutput, calls=%fused_computation.37 | convolution fusion | flops 8153726976 | bytes 14450688 | tf_op jit(solution)/shard_map/ngd,gkd->gnk/dot_general | solution.py:61
  392.1 0.0 copy-done.1
  392.1 0.0 copy-done.3
  392.1 12.7 %fusion.18 = f32[2,288,1152]{2,1,0:T(8,128)} fusion(f32[1024,2,1152]{2,0,1:T(8,128)S(1)} %copy-done.1, f32[2,288,1024]{2,1,0:T(8,128)S(1)} %copy-done.3), kind=kOutput, calls=%fused_computation.25 | convolution fusion | flops 8158445568 | bytes 14450688 | tf_op jit(solution)/shard_map/gnk,ngd->gkd/dot_general | solution.py:60
  404.8 13.8 %fusion = f32[2,288,1152]{2,1,0:T(8,128)} fusion(f32[1024,1152]{1,0:T(8,128)} %all-gather.7.cloned.1.call-done, f32[2,1024,288]{1,2,0:T(8,128)S(1)} %fusion.31, f32[2,288,1024]{2,1,0:T(8,128)S(1)} %copy-done.3), kind=kOutput, calls=%fused_computation.4 | convolution fusion | flops 8156676096 | bytes 12091392 | tf_op jit(solution)/shard_map/gnk,nd->gkd/dot_general | solution.py:62
  (3 shorter events, 0.0 us)
Async XLA Ops:
  7.2 73.2 %copy-start = (f32[2,288,1152]{2,1,0:T(8,128)S(1)}, f32[2,288,1152]{2,1,0:T(8,128)}, u32[]{:S(2)}) copy-start(f32[2,288,1152]{2,1,0:T(8,128)} %param.9) | copy-start | bytes 7962628
  7.2 59.2 %all-gather.7.cloned.1.call-start = ((), (), s32[]{:S(2)}) async-start(), calls=%async_computation.1 | async-start | bytes 4866048 | tf_op jit(solution)/shard_map/all_gather | solution.py:40
  7.9 212.0 %reduce-scatter.4.cloned.1.call-start = ((), (), s32[]{:S(2)}) async-start(), calls=%async_computation.5 | async-start | bytes 9732096
  78.9 1.4 copy-start.2
  119.4 140.3 %all-gather.11.cloned.1.call-start = ((), (), s32[]{:S(2)}) async-start(), calls=%async_computation.3 | async-start | bytes 1327104 | tf_op jit(solution)/shard_map/all_gather | solution.py:11
  223.7 43.8 %copy-start.4 = (f32[32,1152]{1,0:T(8,128)S(1)}, f32[32,1152]{1,0:T(8,128)}, u32[]{:S(2)}) copy-start(f32[32,1152]{1,0:T(8,128)} %param.7) | copy-start | bytes 442372
  224.6 81.2 %all-gather.13.cloned.1.call-start = ((), (), s32[]{:S(2)}) async-start(), calls=%async_computation.4 | async-start | bytes 1327104 | tf_op jit(solution)/shard_map/all_gather | solution.py:11
  268.5 110.2 %all-gather.9.cloned.1.call-start = ((), (), s32[]{:S(2)}) async-start(), calls=%async_computation.2 | async-start | bytes 9732096 | tf_op jit(solution)/shard_map/all_gather | solution.py:58
  378.7 13.4 %copy-start.1 = (f32[1024,2,1152]{2,0,1:T(8,128)S(1)}, f32[1024,2,1152]{2,0,1:T(8,128)}, u32[]{:S(2)}) copy-start(f32[1024,2,1152]{2,0,1:T(8,128)} %all-gather.9.cloned.1.call-done) | copy-start | bytes 28311556
  378.7 13.4 %copy-start.3 = (f32[2,288,1024]{2,1,0:T(8,128)S(1)}, f32[2,288,1024]{2,1,0:T(8,128)}, u32[]{:S(2)}) copy-start(f32[2,288,1024]{2,1,0:T(8,128)} %copy-done.2) | copy-start | bytes 7077892
Sparse Core Ops, SparseCore 0:
  10.5 55.8 all-gather.6
  119.5 100.3 reduce-scatter.3
  224.7 34.9 all-gather.10
  268.6 37.2 all-gather.12
  314.6 64.0 all-gather.8
where the time goes:
time: 430 us; the launch traced here: 425 us
  waiting for transfers between devices  282 us (66%)
  matrix products  72.2 us (17%)
  other arithmetic  30.9 us (7%)
  local copies, waits for them, and re-layouts  25.5 us (6%)
  between operations  14.1 us (3%)
    unnamed x6, waiting for transfers between devices  101 us
    all_gather x1, waiting for transfers between devices, per_device(): suffix_piece = lax.all_gather(suffix, 'feat', axis=0, tiled=True)  64.2 us
    all_gather x1, waiting for transfers between devices, per_device(): gathered = lax.all_gather(activations, 'feat', axis=0, tiled=True)  58.4 us
    all_gather x2, waiting for transfers between devices, entering(): everything = lax.all_gather(shard, axis)  58.2 us
    dot_general x1, matrix products, per_device(): jnp.einsum('gnk,gkd->ngd', feat_rows, dec_weight, precision=HIGHEST)  19.8 us
    select_n x16, other arithmetic, step(): return jnp.where(reached, new, before)  15.3 us
    unnamed x13, local copies, waits for them, and re-layouts  14.3 us
    dot_general x1, matrix products, per_device(): jnp.einsum('gnk,nd->gkd', gate, gathered, precision=HIGHEST)  13.8 us
  transfers between devices with their start and end apart: 5, of which 5 were waited for; matrix products, arithmetic and copies ran while one was open for 3% of the time, Pallas kernels for 0%

commit v1 on v0

--- a/solution.py
+++ b/solution.py
@@ -55,7 +55,9 @@
     )
     decoded = summed.reshape(summed.shape[0], local_groups, model_width)
     suffix = factor * chain_scan(decoded, activations)
-    suffix_piece = lax.all_gather(suffix, "feat", axis=0, tiled=True)
+    suffix_piece = jnp.concatenate(
+        lax.all_to_all(jnp.stack([suffix] * lax.axis_size("feat")), "feat", 0, 0), axis=0
+    )
     feat_rows = features
     dec_new = empty + jnp.einsum("gnk,ngd->gkd", feat_rows, suffix_piece, precision=HIGHEST)
     gate = jnp.einsum("ngd,gkd->gnk", suffix_piece, dec_weight, precision=HIGHEST) * slopes

time: 430 us -> 485 us (1.13)
  blocking collectives: 0 us -> 119 us
  waiting for transfers between devices: 282 us -> 230 us
  other arithmetic: 30.9 us -> 18.2 us
  local copies, waits for them, and re-layouts: 25.5 us -> 31 us
  matrix products: 72.2 us -> 66.8 us
    all_to_all x0 -> x1, blocking collectives: none -> 119 us  [per_device(): lax.all_to_all(jnp.stack([suffix] * lax.axis_size('feat')), 'feat', 0, 0)]
    all_gather x1 -> x0, waiting for transfers between devices: 64.2 us -> none  [per_device(): suffix_piece = lax.all_gather(suffix, 'feat', axis=0, tiled=True)]
    all_gather x2, waiting for transfers between devices: 58.2 us -> 70.2 us  [entering(): everything = lax.all_gather(shard, axis)]
    another operation x1, other arithmetic: 12.6 us -> 0.54 us  [chain_scan(): jnp.cumsum(jnp.flip(errors, 1), axis=1)]
    unnamed x6 -> x5, waiting for transfers between devices: 101 us -> 101 us
    unnamed x13 -> x15, local copies, waits for them, and re-layouts: 14.3 us -> 14.3 us
  transfers between devices with their start and end apart: 5 -> 4, of which waited for: 5 -> 4; matrix products, arithmetic and copies ran while one was open for 3% -> 0% of each run, Pallas kernels for 0% -> 0%
where the time goes in v1:
time: 485 us; the launch traced here: 480 us
  waiting for transfers between devices  230 us (47%)
  blocking collectives  119 us (25%)
  matrix products  66.8 us (14%)
  local copies, waits for them, and re-layouts  31 us (6%)
  other arithmetic  18.2 us (4%)
  between operations  14.1 us (3%)
    all_to_all x1, blocking collectives, per_device(): lax.all_to_all(jnp.stack([suffix] * lax.axis_size('feat')), 'feat', 0, 0)  119 us
    unnamed x5, waiting for transfers between devices  101 us
    all_gather x2, waiting for transfers between devices, entering(): everything = lax.all_gather(shard, axis)  70.2 us
    all_gather x1, waiting for transfers between devices, per_device(): gathered = lax.all_gather(activations, 'feat', axis=0, tiled=True)  58.4 us
    dot_general x1, matrix products, per_device(): jnp.einsum('gnk,gkd->ngd', feat_rows, dec_weight, precision=HIGHEST)  19.6 us
    select_n x16, other arithmetic, step(): return jnp.where(reached, new, before)  15.3 us
    unnamed x15, local copies, waits for them, and re-layouts  14.3 us
    dot_general x1, matrix products, per_device(): jnp.einsum('gnk,ngd->gkd', feat_rows, suffix_piece, precision=HIGHEST)  13.1 us
  transfers between devices with their start and end apart: 4, of which 4 were waited for; matrix products, arithmetic and copies ran while one was open for 0% of the time, Pallas kernels for 0%

profile of v1, /device:TPU:1, one launch (start us, length us, event | category | flops | bytes accessed | tf_op | source)
XLA Modules:
  0.0 479.8 jit_solution(15696266315157196767)
XLA Ops:
  7.2 0.0 copy-start
  7.2 0.0 all-gather.6.cloned.1.call-start
  7.2 0.7 all-gather.6.cloned.1.call-update
  7.9 0.0 reduce-scatter.4.cloned.1.call-start
  8.0 58.4 %all-gather.6.cloned.1.call-done = f32[1024,1152]{1,0:T(8,128)} async-done(((f32[32,1152]{1,0:T(8,128)}), f32[1024,1152]{1,0:T(8,128)}) %all-gather.6.cloned.1.call-update) | async-done | bytes 4718608 | tf_op jit(solution)/shard_map/all_gather | solution.py:40
  66.4 12.5 %fusion.2 = f32[2,288,1024]{2,1,0:T(8,128)S(1)} fusion(f32[2,288,1152]{2,1,0:T(8,128)} %param.8, f32[1024,1152]{1,0:T(8,128)} %all-gather.6.cloned.1.call-done), kind=kOutput, calls=%fused_computation.6 | convolution fusion | flops 8153726976 | bytes 9732096 | tf_op jit(solution)/shard_map/nd,gkd->gnk/dot_general | solution.py:42
  78.9 0.0 copy-start.1
  78.9 1.4 copy-done.1
  80.3 0.0 copy-done
  80.3 19.6 %convolution_bitcast_fusion = f32[1024,2,1152]{2,0,1:T(8,128)} fusion(f32[2,288,1152]{2,1,0:T(8,128)S(1)} %copy-done, f32[2,288,1024]{2,1,0:T(8,128)S(1)} %fusion.2), kind=kOutput, calls=%fused_computation.3 | convolution fusion | flops 8158445568 | bytes 14450688 | tf_op jit(solution)/shard_map/gnk,gkd->ngd/dot_general | solution.py:49
  99.9 9.6 %copy.12 = f32[1024,2,1152]{0,2,1:T(8,128)} copy(f32[1024,2,1152]{2,0,1:T(8,128)} %convolution_bitcast_fusion) | data formatting | bytes 18874368 | tf_op jit(solution)/shard_map/gnk,gkd->ngd/transpose | solution.py:49
  109.6 9.6 %copy.18 = f32[1024,2304]{1,0:T(8,128)} copy(f32[1024,2304]{0,1:T(8,128)} %bitcast.58) | data formatting | bytes 18874368
  119.2 0.0 reduce-scatter.4.cloned.1.call-update
  119.2 0.0 all-gather.8.cloned.1.call-start
  119.3 100.5 %reduce-scatter.4.cloned.1.call-done = f32[32,2304]{1,0:T(8,128)} async-done(((f32[1024,2304]{1,0:T(8,128)}), f32[32,2304]{1,0:T(8,128)}) %reduce-scatter.4.cloned.1.call-update) | async-done | bytes 294928
  219.7 2.3 copy.19
  222.1 1.4 reduce_sum.18
  223.5 0.0 copy-start.3
  223.5 0.9 copy.20
  224.4 0.0 all-gather.8.cloned.1.call-update
  224.4 0.0 all-gather.10.cloned.1.call-start
  224.5 1.6 copy.14
  226.1 33.4 %all-gather.8.cloned.1.call-done = f32[256,1152]{1,0:T(8,128)} async-done(((f32[32,1152]{1,0:T(8,128)}), f32[256,1152]{1,0:T(8,128)}) %all-gather.8.cloned.1.call-update) | async-done | bytes 1179664 | tf_op jit(solution)/shard_map/all_gather | solution.py:11
  259.5 7.8 %while.30 = (s32[]{:T(128)}, f32[32,1152]{1,0:T(8,128)S(1)}, s32[]{:T(128)}, f32[8,32,1152]{2,1,0:T(8,128)}, s32[]{:T(128)}, /*index=5*/s32[]{:T(128)}) while((s32[]{:T(128)}, f32[32,1152]{1,0:T(8,128)S(1)}, s32[]{:T(128)}, f32[8,32,1152]{2,1,0:T(8,128)}, s32[]{:T(128)}, /*index=5*/s32[]{:T(128)}) %tuple.87), condition=%wide.region_3.4_spmd.clone, body=%wide.region_2.3_spmd.clone.sunk | while | flops 110596 | bytes 442461 | solution.py:20
  259.5 1.0 add_select_fusion.4
  260.5 1.0 add_select_fusion.4
  261.5 1.0 add_select_fusion.4
  262.4 1.0 add_select_fusion.4
  263.4 1.0 add_select_fusion.4
  264.4 1.0 add_select_fusion.4
  265.4 1.0 add_select_fusion.4
  266.4 1.0 add_select_fusion.4
  267.3 0.0 copy-done.3
  267.3 0.9 fusion.29
  268.2 0.0 all-gather.10.cloned.1.call-update
  268.3 0.5 fusion.30
  268.8 36.8 %all-gather.10.cloned.1.call-done = f32[256,1152]{1,0:T(8,128)} async-done(((f32[32,1152]{1,0:T(8,128)}), f32[256,1152]{1,0:T(8,128)}) %all-gather.10.cloned.1.call-update) | async-done | bytes 1179664 | tf_op jit(solution)/shard_map/all_gather | solution.py:11
  305.6 7.9 %while.31 = (s32[]{:T(128)}, f32[32,1152]{1,0:T(8,128)S(1)}, s32[]{:T(128)}, f32[8,32,1152]{2,1,0:T(8,128)}, s32[]{:T(128)}, /*index=5*/s32[]{:T(128)}, s32[]{:T(128)}, s32[]{:T(128)}) while((s32[]{:T(128)}, f32[32,1152]{1,0:T(8,128)S(1)}, s32[]{:T(128)}, f32[8,32,1152]{2,1,0:T(8,128)}, s32[]{:T(128)}, /*index=5*/s32[]{:T(128)}, ...), condition=%wide.region_7.8_spmd.clone, body=%wide.region_6.7_spmd.clone.sunk | while | flops 110600 | bytes 442523 | solution.py:20
  305.6 1.0 add_select_fusion.5
  306.6 1.0 add_select_fusion.5
  307.6 1.0 add_select_fusion.5
  308.6 1.0 add_select_fusion.5
  309.6 1.0 add_select_fusion.5
  310.6 1.0 add_select_fusion.5
  311.6 1.0 add_select_fusion.5
  312.6 1.0 add_select_fusion.5
  313.6 1.1 stack.2
  314.7 119.4 %all_to_all.5 = f32[32,32,2,1152]{3,1,2,0:T(8,128)} all-to-all(f32[32,32,2,1152]{3,1,2,0:T(8,128)S(1)} %stack.2), channel_id=1, replica_groups=mesh['prefix'=8,'feat'=32] {'feat'}, dimensions={0} | all-to-all | bytes 18874368 | tf_op jit(solution)/shard_map/all_to_all | solution.py:59
  434.1 4.3 copy.15
  438.4 0.0 copy-start.2
  438.4 0.0 slice-start
  438.4 10.1 %fusion.31 = f32[2,1024,288]{1,2,0:T(8,128)S(1)} fusion(f32[1024,2,1152]{2,0,1:T(8,128)S(1)} %bitcast.56, f32[2,288,1152]{2,1,0:T(8,128)S(1)} %copy-done), kind=kOutput, calls=%fused_computation.37 | convolution fusion | flops 8153726976 | bytes 14450688 | tf_op jit(solution)/shard_map/ngd,gkd->gnk/dot_general | solution.py:63
  448.5 0.0 copy-done.2
  448.5 0.0 slice-start.1
  448.5 13.1 %fusion.18 = f32[2,288,1152]{2,1,0:T(8,128)} fusion(f32[1024,2,1152]{2,0,1:T(8,128)S(1)} %bitcast.57, f32[2,288,1024]{2,1,0:T(8,128)S(1)} %copy-done.2), kind=kOutput, calls=%fused_computation.25 | convolution fusion | flops 8158445568 | bytes 14450688 | tf_op jit(solution)/shard_map/gnk,ngd->gkd/dot_general | solution.py:62
  461.6 0.0 slice-done
  461.6 0.0 slice-done.1
  461.6 11.5 %fusion = f32[2,288,1152]{2,1,0:T(8,128)} fusion(f32[1024,1152]{1,0:T(8,128)S(1)} %bitcast.62, f32[2,1024,288]{1,2,0:T(8,128)S(1)} %fusion.31, f32[2,288,1024]{2,1,0:T(8,128)S(1)} %copy-done.2), kind=kOutput, calls=%fused_computation.4 | convolution fusion | flops 8156676096 | bytes 12091392 | tf_op jit(solution)/shard_map/gnk,nd->gkd/dot_general | solution.py:64
  (5 shorter events, 0.1 us)
Async XLA Ops:
  7.2 73.2 %copy-start = (f32[2,288,1152]{2,1,0:T(8,128)S(1)}, f32[2,288,1152]{2,1,0:T(8,128)}, u32[]{:S(2)}) copy-start(f32[2,288,1152]{2,1,0:T(8,128)} %param.9) | copy-start | bytes 7962628
  7.2 59.2 %all-gather.6.cloned.1.call-start = ((), (), s32[]{:S(2)}) async-start(), calls=%async_computation.2 | async-start | bytes 4866048 | tf_op jit(solution)/shard_map/all_gather | solution.py:40
  7.9 211.8 %reduce-scatter.4.cloned.1.call-start = ((), (), s32[]{:S(2)}) async-start(), calls=%async_computation.5 | async-start | bytes 9732096
  78.9 1.4 copy-start.1
  119.2 140.3 %all-gather.8.cloned.1.call-start = ((), (), s32[]{:S(2)}) async-start(), calls=%async_computation.3 | async-start | bytes 1327104 | tf_op jit(solution)/shard_map/all_gather | solution.py:11
  223.5 43.8 %copy-start.3 = (f32[32,1152]{1,0:T(8,128)S(1)}, f32[32,1152]{1,0:T(8,128)}, u32[]{:S(2)}) copy-start(f32[32,1152]{1,0:T(8,128)} %param.7) | copy-start | bytes 442372
  224.4 81.3 %all-gather.10.cloned.1.call-start = ((), (), s32[]{:S(2)}) async-start(), calls=%async_computation.4 | async-start | bytes 1327104 | tf_op jit(solution)/shard_map/all_gather | solution.py:11
  438.4 10.1 %copy-start.2 = (f32[2,288,1024]{2,1,0:T(8,128)S(1)}, f32[2,288,1024]{2,1,0:T(8,128)}, u32[]{:S(2)}) copy-start(f32[2,288,1024]{2,1,0:T(8,128)} %copy-done.1) | copy-start | bytes 7077892
  438.4 23.2 %slice-start = ((s8[4718592]{0:T(1024)(128)(4,1)}), s8[4194304]{0:T(1024)(128)(4,1)S(1)}, s32[]{:S(2)}) async-start(s8[4718592]{0:T(1024)(128)(4,1)} %bitcast.61), calls=%async_computation.6 | async-start | bytes 8388608
  448.5 13.1 %slice-start.1 = ((s8[4718592]{0:T(1024)(128)(4,1)}), s8[524288]{0:T(1024)(128)(4,1)S(1)}, s32[]{:S(2)}) async-start(s8[4718592]{0:T(1024)(128)(4,1)} %bitcast.61), calls=%async_computation.7 | async-start | bytes 1048576
Sparse Core Ops, SparseCore 0:
  10.5 55.8 all-gather.5
  119.3 100.3 reduce-scatter.3
  224.5 34.9 all-gather.7
  268.4 37.2 all-gather.9
